TPU v7x, 512 devices: a whole 4x4x16 slice. The times are simulated.
512 devices in a mesh: feat: 8 (over z_lo), lat: 64 (over y, z_hi, x, core).
Axes of the slice: x: 4, y: 4, z: 16 (z_hi: 2, z_lo: 8; z = z_hi * 8 + z_lo), core: 2. Of those that a mesh axis runs over, the one named last changes fastest.
Arguments:
- acts: bfloat16 [2, 512, 4096], P(None, 'lat', 'feat'), may hold values from -6 to 6
- weight: bfloat16 [2, 4096, 65536], P(None, 'feat', 'lat'), may hold values from -0.0625 to 0.0625
- enc_bias: float32 [65536], P('lat'), may hold values from -1 to 0.5
- dec_bias: float32 [2, 4096], P(None, 'feat'), may hold values from -1 to 1
Outputs:
- grad_weight: bfloat16 [2, 4096, 65536], P(None, 'feat', 'lat')
- grad_enc_bias: float32 [65536], P('lat')
- grad_dec_bias: float32 [2, 4096], P(None, 'feat')
All inputs are finite; a program needn't handle non-finite values.
Results may differ from a plain program's by a relative error of at most 0.0085.
Values may be sent and summed in bfloat16 or wider, within the bound.
A program may use at most 64 MiB of HBM per device.

v0:
```python
import math
import jax
import jax.numpy as jnp
from jax import lax
from jax.sharding import Mesh
from jax.sharding import PartitionSpec as P

LAT = ("lat_0", "lat_1", "lat_2", "lat_3")


def in_blocks(shard, dim, count):
    dims = shard.shape
    blocks = shard.reshape(*dims[:dim], count, dims[dim] // count, *dims[dim + 1 :])
    return jnp.moveaxis(blocks, dim, 0)


def summed_on_arrival(shard, axis, dim):
    blocks = in_blocks(shard, dim, lax.axis_size(axis))
    arrived = lax.all_to_all(blocks, axis, split_axis=0, concat_axis=0, tiled=True)
    return arrived.astype(jnp.float32).sum(axis=0)


def in_order(blocks, dim):
    dims = list(blocks.shape[1:])
    dims[dim] *= blocks.shape[0]
    return jnp.moveaxis(blocks, 0, dim).reshape(dims)


def from_everyone(shard, axis):
    copies = jnp.broadcast_to(shard, (lax.axis_size(axis), *shard.shape))
    return lax.all_to_all(copies, axis, split_axis=0, concat_axis=0, tiled=True)


def gathered_copies(shard, axis, dim):
    return in_order(from_everyone(shard, axis), dim)


def sum_at_owner(shard, axis, dim):
    count = lax.axis_size(axis)
    blocks = lax.all_to_all(in_blocks(shard, dim, count), axis, 0, 0, tiled=True)
    return jnp.sum(blocks, axis=0)


def sum_by_axis(shard, axes, dim):
    far, near = axes
    blocks = in_blocks(shard, dim, lax.axis_size(far))
    nearer = sum_at_owner(blocks, near, dim + 1)
    arrived = lax.all_to_all(nearer, far, split_axis=0, concat_axis=0, tiled=True)
    return arrived.sum(axis=0)


def filled_up(lines, count):
    spare = -len(lines) % count
    return jnp.pad(lines, [(0, spare)] + [(0, 0)] * (lines.ndim - 1))


def gathered_by_axis(shard, axes, dim):
    far, near = axes
    blocks = from_everyone(from_everyone(shard, far), near)
    return in_order(blocks.swapaxes(0, 1).reshape(-1, *shard.shape), dim)


def nested_sum(shard, axes):
    lines = shard.reshape(-1, shard.shape[-1])
    own = sum_by_axis(filled_up(lines, lax.axis_size(axes[0]) * lax.axis_size(axes[1])), axes, 0)
    whole = gathered_by_axis(own, axes, 0)
    return whole[: len(lines)].reshape(shard.shape)


def taken_together(shard, axis):
    everything = from_everyone(shard, axis)
    return jnp.sum(everything, axis=0)


def channel_terms(left, right):
    first = jnp.dot(left[0], right[0], preferred_element_type=jnp.float32)
    return first + jnp.dot(left[1], right[1], preferred_element_type=jnp.float32)


def on_device(acts, weight, enc_bias, dec_bias):
    width = weight.shape[1] * lax.axis_size("feat")
    lats = weight.shape[2] * lax.axis_size(LAT)
    scale = math.sqrt(2.0 * width / lats)
    whole_rows = lax.all_gather(acts, LAT, axis=1, tiled=True)
    partial_value = channel_terms(whole_rows, weight)
    pre_share = summed_on_arrival(partial_value.astype(jnp.bfloat16), "feat", 0) + enc_bias
    act_share = jax.nn.softplus(pre_share).astype(jnp.bfloat16)
    latents = gathered_copies(act_share, "feat", 0)
    recon_terms = jnp.einsum("rl,mdl->mrd", latents, weight, preferred_element_type=jnp.float32)
    summed = nested_sum(recon_terms, (("lat_0", "lat_1", "lat_2"), "lat_3"))
    resid = scale * summed + dec_bias[:, None, :] - whole_rows.astype(jnp.float32)
    grad_dec_bias = jnp.sum(resid, axis=1)
    resid_rows = resid.astype(jnp.bfloat16)
    backed = channel_terms(resid_rows, weight)
    back_part = summed_on_arrival(backed.astype(jnp.bfloat16), "feat", 0)
    grad_share = scale * back_part * jax.nn.sigmoid(pre_share)
    grad_enc_bias = taken_together(jnp.sum(grad_share, axis=0), "feat")
    grad_pre_b = gathered_copies(grad_share.astype(jnp.bfloat16), "feat", 0)
    enc_term = jnp.einsum("mrd,rl->mdl", whole_rows, grad_pre_b, preferred_element_type=jnp.float32)
    dec_term = jnp.einsum("mrd,rl->mdl", resid_rows, latents, preferred_element_type=jnp.float32)
    grad_weight = (enc_term + scale * dec_term).astype(jnp.bfloat16)
    return (grad_weight, grad_enc_bias, grad_dec_bias)


def solution(mesh):
    torus = Mesh(
        mesh.devices.reshape(mesh.shape["feat"], 4, 2, 4, 2),
        ("feat", "lat_0", "lat_1", "lat_2", "lat_3"),
    )
    in_specs = (P(None, LAT, "feat"), P(None, "feat", LAT), P(LAT), P(None, "feat"))
    out_specs = (P(None, "feat", LAT), P(LAT), P(None, "feat"))
    return jax.shard_map(
        on_device, mesh=torus, in_specs=in_specs, out_specs=out_specs, check_vma=False
    )
```

profile of v0, /device:TPU:2, one launch (start us, length us, event | category | flops | bytes accessed | tf_op | source)
XLA Modules:
  0.0 509.9 jit_solution(4687224585062646519)
XLA Ops:
  7.2 0.0 copy-start.1
  7.2 0.0 all-gather.2.cloned.1.call-start
  7.2 0.7 all-gather.2.cloned.1.call-update
  7.9 110.8 %all-gather.2.cloned.1.call-done = bf16[2,512,512]{2,1,0:T(8,128)(2,1)} async-done(((bf16[2,8,512]{2,1,0:T(8,128)(2,1)}), bf16[2,512,512]{2,1,0:T(8,128)(2,1)}) %all-gather.2.cloned.1.call-update) | async-done | bytes 1048592 | tf_op jit(solution)/shard_map/all_gather | solution.py:84
  118.8 0.0 copy-start
  118.8 2.2 fusion.7
  120.9 0.0 copy-done.1
  121.0 0.0 copy-done
  121.0 0.7 add_convert_fusion.1
  121.7 0.0 copy-start.5
  121.7 54.3 %all_to_all.46 = bf16[8,64,1024]{2,1,0:T(8,128)(2,1)S(1)} all-to-all(bf16[8,64,1024]{2,1,0:T(8,128)(2,1)S(1)} %bitcast.52), channel_id=1, replica_groups=mesh['feat'=8,'lat_0'=4,'lat_1'=2,'lat_2'=4,'lat_3'=2] {'feat'}, dimensions={0} | all-to-all | bytes 2097152 | tf_op jit(solution)/shard_map/all_to_all | solution.py:19
  176.0 0.2 convert_reduce_fusion.1
  176.2 0.0 copy-done.5
  176.2 0.2 fusion.13
  176.3 0.1 broadcast_in_dim.17
  176.5 55.2 %all_to_all.47 = bf16[8,64,1024]{2,1,0:T(8,128)(2,1)S(1)} all-to-all(bf16[8,64,1024]{2,1,0:T(8,128)(2,1)S(1)} %broadcast_in_dim.17), channel_id=1, replica_groups=mesh['feat'=8,'lat_0'=4,'lat_1'=2,'lat_2'=4,'lat_3'=2] {'feat'}, dimensions={0} | all-to-all | bytes 2097152 | tf_op jit(solution)/shard_map/all_to_all | solution.py:31
  231.7 0.0 copy-start.3
  231.7 1.3 fusion.15
  233.0 0.0 copy-done.3
  233.0 0.3 copy.40
  233.3 5.4 %all_to_all.48 = f32[2,32,16,512]{3,2,1,0:T(8,128)S(1)} all-to-all(f32[2,32,16,512]{3,2,1,0:T(8,128)S(1)} %bitcast.50), channel_id=1, replica_groups=mesh['feat'=8,'lat_0'=4,'lat_1'=2,'lat_2'=4,'lat_3'=2] {'lat_3'}, dimensions={0} | all-to-all | bytes 4194304 | tf_op jit(solution)/shard_map/all_to_all | solution.py:40
  238.7 1.3 reduce_sum.64
  239.9 60.7 %all_to_all.49 = f32[32,16,512]{2,1,0:T(8,128)S(1)} all-to-all(f32[32,16,512]{2,1,0:T(8,128)} %reduce_sum.64), channel_id=1, replica_groups=mesh['feat'=8,'lat_0'=4,'lat_1'=2,'lat_2'=4,'lat_3'=2] {'lat_0','lat_1',..., dimensions={0} | all-to-all | bytes 2097152 | tf_op jit(solution)/shard_map/all_to_all | solution.py:48
  300.6 0.1 reduce_sum.65
  300.7 0.1 broadcast_in_dim.18
  300.8 50.3 %all_to_all.50 = f32[32,16,512]{2,1,0:T(8,128)S(1)} all-to-all(f32[32,16,512]{2,1,0:T(8,128)S(1)} %broadcast_in_dim.18), channel_id=1, replica_groups=mesh['feat'=8,'lat_0'=4,'lat_1'=2,'lat_2'=4,'lat_3'=2] {'lat_0','lat_1',..., dimensions={0} | all-to-all | bytes 2097152 | tf_op jit(solution)/shard_map/all_to_all | solution.py:31
  351.1 0.3 broadcast_in_dim.19
  351.3 5.4 %all_to_all.51 = f32[2,32,16,512]{3,2,1,0:T(8,128)S(1)} all-to-all(f32[2,32,16,512]{3,2,1,0:T(8,128)S(1)} %broadcast_in_dim.19), channel_id=1, replica_groups=mesh['feat'=8,'lat_0'=4,'lat_1'=2,'lat_2'=4,'lat_3'=2] {'lat_3'}, dimensions={0} | all-to-all | bytes 4194304 | tf_op jit(solution)/shard_map/all_to_all | solution.py:31
  356.8 0.2 multiply_bitcast_fusion
  357.0 0.0 copy-start.6
  357.0 0.3 copy.28
  357.3 0.4 copy-done.6
  357.7 1.0 fusion.1
  358.7 0.6 copy-done.2
  359.3 0.7 fusion.5
  360.0 0.7 add_convert_fusion
  360.7 65.0 %all_to_all.52 = bf16[8,64,1024]{2,1,0:T(8,128)(2,1)S(1)} all-to-all(bf16[8,64,1024]{2,1,0:T(8,128)(2,1)S(1)} %bitcast.53), channel_id=1, replica_groups=mesh['feat'=8,'lat_0'=4,'lat_1'=2,'lat_2'=4,'lat_3'=2] {'feat'}, dimensions={0} | all-to-all | bytes 2097152 | tf_op jit(solution)/shard_map/all_to_all | solution.py:19
  425.7 0.2 convert_reduce_fusion
  425.9 0.1 fusion.14
  426.0 14.7 %all_to_all.53 = f32[8,1,1024]{2,1,0:T(1,128)S(1)} all-to-all(f32[8,1,1024]{2,1,0:T(1,128)S(1)} %broadcast_in_dim.21), channel_id=1, replica_groups=mesh['feat'=8,'lat_0'=4,'lat_1'=2,'lat_2'=4,'lat_3'=2] {'feat'}, dimensions={0} | all-to-all | bytes 65536 | tf_op jit(solution)/shard_map/all_to_all | solution.py:31
  440.7 1.1 broadcast_in_dim.20
  441.8 3.6 all-to-all-start.7
  445.4 0.6 reduce_sum.68
  446.0 49.1 %all-to-all-done.7 = bf16[8,64,1024]{2,1,0:T(8,128)(2,1)S(1)} async-done(((bf16[8,64,1024]{2,1,0:T(8,128)(2,1)}), bf16[8,64,1024]{2,1,0:T(8,128)(2,1)S(1)}, u32[]{:S(2)}, u32[]{:S(2)}) %all-to-all-start.7) | async-done | bytes 1048608 | tf_op jit(solution)/shard_map/all_to_all | solution.py:31
  495.1 1.3 fusion.16
  496.4 0.0 copy-done.4
  496.4 2.8 fusion
  499.1 3.9 copy.33
  (3 shorter events, 0.0 us)
Async XLA Ops:
  7.2 113.8 %copy-start.1 = (bf16[2,512,1024]{2,1,0:T(8,128)(2,1)S(1)}, bf16[2,512,1024]{2,1,0:T(8,128)(2,1)}, u32[]{:S(2)}) copy-start(bf16[2,512,1024]{2,1,0:T(8,128)(2,1)} %param.5) | copy-start | bytes 6291460
  7.2 111.6 %all-gather.2.cloned.1.call-start = ((), (), s32[]{:S(2)}) async-start(), calls=%async_computation.9 | async-start | bytes 1064960 | tf_op jit(solution)/shard_map/all_gather | solution.py:84
  118.8 2.2 copy-start
  121.7 54.5 %copy-start.5 = (f32[1024]{0:T(1024)S(1)}, f32[1024]{0:T(1024)}, u32[]{:S(2)}) copy-start(f32[1024]{0:T(1024)} %param.6) | copy-start | bytes 12292
  231.7 1.3 copy-start.3
  357.0 0.7 copy-start.6
  357.7 1.6 copy-start.2
  441.8 53.3 %all-to-all-start.7 = ((bf16[8,64,1024]{2,1,0:T(8,128)(2,1)}), bf16[8,64,1024]{2,1,0:T(8,128)(2,1)S(1)}, u32[]{:S(2)}, u32[]{:S(2)}) async-start(bf16[8,64,1024]{2,1,0:T(8,128)(2,1)} %broadcast_in_dim.20), calls=%async_computation.7 | async-start | bytes 2097152 | tf_op jit(solution)/shard_map/all_to_all | solution.py:31
  495.1 1.3 copy-start.4
Sparse Core Ops, SparseCore 0:
  12.2 106.4 all-gather.1
where the time goes:
time: 511 us; the launch traced here: 510 us
  blocking collectives  311 us (61%)
  waiting for transfers between devices  161 us (32%)
  between operations  14.2 us (3%)
  matrix products  9.68 us (2%)
  local copies, waits for them, and re-layouts  7.09 us (1%)
    all_to_all x4, blocking collectives, from_everyone(): return lax.all_to_all(copies, axis, split_axis=0, concat_axis=0, tiled=True)  126 us
    all_to_all x2, blocking collectives, summed_on_arrival(): lax.all_to_all(blocks, axis, split_axis=0, concat_axis=0, tiled=True)  119 us
    all_gather x1, waiting for transfers between devices, on_device(): whole_rows = lax.all_gather(acts, LAT, axis=1, tiled=True)  111 us
    all_to_all x1, blocking collectives, sum_by_axis(): lax.all_to_all(nearer, far, split_axis=0, concat_axis=0, tiled=True)  60.7 us
    all_to_all x1, waiting for transfers between devices, from_everyone(): return lax.all_to_all(copies, axis, split_axis=0, concat_axis=0, tiled=True)  49.1 us
  transfers between devices with their start and end apart: 2, of which 2 were waited for; matrix products, arithmetic and copies ran while one was open for 0% of the time, Pallas kernels for 0%

commit v1 on v0

--- a/solution.py
+++ b/solution.py
@@ -81,7 +81,8 @@
     width = weight.shape[1] * lax.axis_size("feat")
     lats = weight.shape[2] * lax.axis_size(LAT)
     scale = math.sqrt(2.0 * width / lats)
-    whole_rows = lax.all_gather(acts, LAT, axis=1, tiled=True)
+    repeated = jnp.stack([acts] * lax.axis_size(LAT))
+    whole_rows = jnp.concatenate(lax.all_to_all(repeated, LAT, 0, 0), axis=1)
     partial_value = channel_terms(whole_rows, weight)
     pre_share = summed_on_arrival(partial_value.astype(jnp.bfloat16), "feat", 0) + enc_bias
     act_share = jax.nn.softplus(pre_share).astype(jnp.bfloat16)

time: 511 us -> 461 us (0.902)
  waiting for transfers between devices: 161 us -> 46.2 us
  blocking collectives: 311 us -> 387 us
  between operations: 14.2 us -> 0.83 us
    all_gather x1 -> x0, waiting for transfers between devices: 111 us -> none  [on_device(): whole_rows = lax.all_gather(acts, LAT, axis=1, tiled=True)]
    all_to_all x0 -> x1, blocking collectives: none -> 52.1 us  [on_device(): whole_rows = jnp.concatenate(lax.all_to_all(repeated, LAT, 0, 0), axis=1)]
    all_to_all x2, blocking collectives: 119 us -> 148 us  [summed_on_arrival(): lax.all_to_all(blocks, axis, split_axis=0, concat_axis=0, tiled=True)]
    all_to_all x1, blocking collectives: 60.7 us -> 55.5 us  [sum_by_axis(): lax.all_to_all(nearer, far, split_axis=0, concat_axis=0, tiled=True)]
  transfers between devices with their start and end apart: 2 -> 1, of which waited for: 2 -> 1; matrix products, arithmetic and copies ran while one was open for 0% -> 1% of each run, Pallas kernels for 0% -> 0%
where the time goes in v1:
time: 461 us; the launch traced here: 460 us
  blocking collectives  387 us (84%)
  waiting for transfers between devices  46.2 us (10%)
  matrix products  8.25 us (2%)
  local copies, waits for them, and re-layouts  7.09 us (2%)
  other arithmetic  5.73 us (1%)
    all_to_all x2, blocking collectives, summed_on_arrival(): lax.all_to_all(blocks, axis, split_axis=0, concat_axis=0, tiled=True)  148 us
    all_to_all x4, blocking collectives, from_everyone(): return lax.all_to_all(copies, axis, split_axis=0, concat_axis=0, tiled=True)  126 us
    all_to_all x1, blocking collectives, sum_by_axis(): lax.all_to_all(nearer, far, split_axis=0, concat_axis=0, tiled=True)  55.5 us
    all_to_all x1, blocking collectives, on_device(): whole_rows = jnp.concatenate(lax.all_to_all(repeated, LAT, 0, 0), axis=1)  52.1 us
    all_to_all x1, waiting for transfers between devices, from_everyone(): return lax.all_to_all(copies, axis, split_axis=0, concat_axis=0, tiled=True)  46.2 us
  transfers between devices with their start and end apart: 1, of which 1 were waited for; matrix products, arithmetic and copies ran while one was open for 1% of the time, Pallas kernels for 0%

profile of v1, /device:TPU:2, one launch (start us, length us, event | category | flops | bytes accessed | tf_op | source)
XLA Modules:
  0.0 459.9 jit_solution(1010326856465870960)
XLA Ops:
  0.6 0.0 copy-start
  0.6 1.0 stack.2
  1.6 52.1 %all_to_all.51 = bf16[64,2,8,512]{3,2,1,0:T(8,128)(2,1)S(1)} all-to-all(bf16[64,2,8,512]{3,2,1,0:T(8,128)(2,1)S(1)} %stack.2), channel_id=1, replica_groups=mesh['feat'=8,'lat_0'=4,'lat_1'=2,'lat_2'=4,'lat_3'=2] {'lat_0','lat_1',..., dimensions={0} | all-to-all | bytes 2097152 | tf_op jit(solution)/shard_map/all_to_all | solution.py:85
  53.8 0.0 copy-done
  53.8 0.7 fusion.7
  54.5 0.7 add_convert_fusion.1
  55.2 0.0 copy-start.6
  55.2 83.2 %all_to_all.52 = bf16[8,64,1024]{2,1,0:T(8,128)(2,1)S(1)} all-to-all(bf16[8,64,1024]{2,1,0:T(8,128)(2,1)S(1)} %bitcast.76), channel_id=1, replica_groups=mesh['feat'=8,'lat_0'=4,'lat_1'=2,'lat_2'=4,'lat_3'=2] {'feat'}, dimensions={0} | all-to-all | bytes 2097152 | tf_op jit(solution)/shard_map/all_to_all | solution.py:19
  138.5 0.2 convert_reduce_fusion.1
  138.6 0.0 copy-done.6
  138.7 0.2 fusion.16
  138.8 0.1 broadcast_in_dim.17
  138.9 54.9 %all_to_all.53 = bf16[8,64,1024]{2,1,0:T(8,128)(2,1)S(1)} all-to-all(bf16[8,64,1024]{2,1,0:T(8,128)(2,1)S(1)} %broadcast_in_dim.17), channel_id=1, replica_groups=mesh['feat'=8,'lat_0'=4,'lat_1'=2,'lat_2'=4,'lat_3'=2] {'feat'}, dimensions={0} | all-to-all | bytes 2097152 | tf_op jit(solution)/shard_map/all_to_all | solution.py:31
  193.8 0.0 copy-start.2
  193.8 1.3 fusion.18
  195.1 0.0 copy-done.2
  195.1 0.3 copy.55
  195.4 5.4 %all_to_all.54 = f32[2,32,16,512]{3,2,1,0:T(8,128)S(1)} all-to-all(f32[2,32,16,512]{3,2,1,0:T(8,128)S(1)} %bitcast.73), channel_id=1, replica_groups=mesh['feat'=8,'lat_0'=4,'lat_1'=2,'lat_2'=4,'lat_3'=2] {'lat_3'}, dimensions={0} | all-to-all | bytes 4194304 | tf_op jit(solution)/shard_map/all_to_all | solution.py:40
  200.8 1.3 reduce_sum.71
  202.1 55.5 %all_to_all.55 = f32[32,16,512]{2,1,0:T(8,128)S(1)} all-to-all(f32[32,16,512]{2,1,0:T(8,128)} %reduce_sum.71), channel_id=1, replica_groups=mesh['feat'=8,'lat_0'=4,'lat_1'=2,'lat_2'=4,'lat_3'=2] {'lat_0','lat_1',..., dimensions={0} | all-to-all | bytes 2097152 | tf_op jit(solution)/shard_map/all_to_all | solution.py:48
  257.6 0.1 reduce_sum.72
  257.7 0.1 broadcast_in_dim.18
  257.8 51.3 %all_to_all.56 = f32[32,16,512]{2,1,0:T(8,128)S(1)} all-to-all(f32[32,16,512]{2,1,0:T(8,128)S(1)} %broadcast_in_dim.18), channel_id=1, replica_groups=mesh['feat'=8,'lat_0'=4,'lat_1'=2,'lat_2'=4,'lat_3'=2] {'lat_0','lat_1',..., dimensions={0} | all-to-all | bytes 2097152 | tf_op jit(solution)/shard_map/all_to_all | solution.py:31
  309.1 0.3 broadcast_in_dim.19
  309.4 5.4 %all_to_all.57 = f32[2,32,16,512]{3,2,1,0:T(8,128)S(1)} all-to-all(f32[2,32,16,512]{3,2,1,0:T(8,128)S(1)} %broadcast_in_dim.19), channel_id=1, replica_groups=mesh['feat'=8,'lat_0'=4,'lat_1'=2,'lat_2'=4,'lat_3'=2] {'lat_3'}, dimensions={0} | all-to-all | bytes 4194304 | tf_op jit(solution)/shard_map/all_to_all | solution.py:31
  314.8 0.2 copy_multiply_fusion
  315.1 0.4 copy-done.5
  315.5 0.4 subtract_convert_fusion
  315.9 1.2 copy-done.1
  317.1 0.7 fusion.5
  317.8 0.7 add_convert_fusion
  318.5 64.7 %all_to_all.58 = bf16[8,64,1024]{2,1,0:T(8,128)(2,1)S(1)} all-to-all(bf16[8,64,1024]{2,1,0:T(8,128)(2,1)S(1)} %bitcast.75), channel_id=1, replica_groups=mesh['feat'=8,'lat_0'=4,'lat_1'=2,'lat_2'=4,'lat_3'=2] {'feat'}, dimensions={0} | all-to-all | bytes 2097152 | tf_op jit(solution)/shard_map/all_to_all | solution.py:19
  383.3 0.2 convert_reduce_fusion
  383.5 0.1 fusion.17
  383.6 14.7 %all_to_all.59 = f32[8,1,1024]{2,1,0:T(1,128)S(1)} all-to-all(f32[8,1,1024]{2,1,0:T(1,128)S(1)} %broadcast_in_dim.21), channel_id=1, replica_groups=mesh['feat'=8,'lat_0'=4,'lat_1'=2,'lat_2'=4,'lat_3'=2] {'feat'}, dimensions={0} | all-to-all | bytes 65536 | tf_op jit(solution)/shard_map/all_to_all | solution.py:31
  398.3 1.1 broadcast_in_dim.20
  399.4 4.4 all-to-all-start.8
  403.8 0.3 bitcast_convert_fusion
  404.1 0.2 copy.34
  404.3 1.7 fusion.14
  406.0 0.6 bitcast_reduce_fusion
  406.6 0.6 reduce_sum.75
  407.2 46.2 %all-to-all-done.8 = bf16[8,64,1024]{2,1,0:T(8,128)(2,1)} async-done(((bf16[8,64,1024]{2,1,0:T(8,128)(2,1)}), bf16[8,64,1024]{2,1,0:T(8,128)(2,1)}, u32[]{:S(2)}, u32[]{:S(2)}) %all-to-all-start.8) | async-done | bytes 1048608 | tf_op jit(solution)/shard_map/all_to_all | solution.py:31
  453.4 2.7 fusion.1
  456.1 0.0 copy-done.3
  456.1 0.0 copy-done.4
  456.1 1.4 fusion
  457.5 2.4 copy.38
  (6 shorter events, 0.0 us)
Async XLA Ops:
  0.6 53.1 %copy-start = (bf16[2,512,1024]{2,1,0:T(8,128)(2,1)S(1)}, bf16[2,512,1024]{2,1,0:T(8,128)(2,1)}, u32[]{:S(2)}) copy-start(bf16[2,512,1024]{2,1,0:T(8,128)(2,1)} %param.5) | copy-start | bytes 6291460
  55.2 83.4 %copy-start.6 = (f32[1024]{0:T(1024)S(1)}, f32[1024]{0:T(1024)}, u32[]{:S(2)}) copy-start(f32[1024]{0:T(1024)} %param.6) | copy-start | bytes 12292
  193.8 1.3 copy-start.2
  314.8 0.7 copy-start.5
  315.5 1.6 copy-start.1
  399.4 54.0 %all-to-all-start.8 = ((bf16[8,64,1024]{2,1,0:T(8,128)(2,1)}), bf16[8,64,1024]{2,1,0:T(8,128)(2,1)}, u32[]{:S(2)}, u32[]{:S(2)}) async-start(bf16[8,64,1024]{2,1,0:T(8,128)(2,1)} %broadcast_in_dim.20), calls=%async_computation.8 | async-start | bytes 2097152 | tf_op jit(solution)/shard_map/all_to_all | solution.py:31
  453.4 2.7 copy-start.3
  453.4 2.7 copy-start.4
